TPU v7x, 32 devices: a whole 2x2x4 slice. The times are simulated.
32 devices in a mesh: grp: 2 (over y), cell: 16 (over z, x, core).
Axes of the slice: x: 2, y: 2, z: 4, core: 2. Of those that a mesh axis runs over, the one named last changes fastest.
Arguments:
- momenta: int32 [3, 65536], replicated, may hold values from 1 to 32
- positions: float32 [3, 4096], P(None, ('grp', 'cell')), parts along dimension 1, may hold values from 0 to 1
- weights: bfloat16 [8, 4096], P(None, ('grp', 'cell')), parts along dimension 1, may hold values from 0.099609375 to 2
- triplets: int32 [3, 16384], P(None, ('grp', 'cell')), parts along dimension 1, may hold values from 0 to 65535, as said below
- cotangent: float32 [8, 16384], P(None, ('grp', 'cell')), parts along dimension 1, may hold values from -6 to 6
Outputs:
- correlation: float32 [8, 16384], P(None, ('grp', 'cell')), parts along dimension 1
- weight_grad: float32 [8, 4096], P(None, ('grp', 'cell')), parts along dimension 1
There are 2 independent parts, one for each index of `grp`. A program takes and returns all parts, laid end to end along the dimension named above; an argument that names none is the same for every part. Nothing has to cross between parts.
Inputs may be any that keep to these rules, and one draw needn't show every extreme that they name: Among the 1536 momentum indices of one device's triplets, each block of 4096 momenta (4096 * r to 4096 * r + 4095) is named either 96 - 1 or 96 times.
All inputs are finite; a program needn't handle non-finite values.
Results may differ from a plain program's by a relative error of at most 0.0051.
Values may be sent and summed in bfloat16 or wider, within the bound.
No kernel may reach another device: no remote copies, remote signals or barrier semaphores. Data moves between devices by JAX's collectives and lax.ppermute only.
A program may use at most 256 MiB of HBM per device.

v0:
```python
import math
import jax
import jax.numpy as jnp
from jax import lax
from jax.sharding import PartitionSpec as P

TWO_PI = 2.0 * math.pi


def tables(moment_block, position_block):
    numbers = moment_block.astype(jnp.float32)
    phase = numbers[0][:, None] * position_block[0][None, :]
    phase = phase + numbers[1][:, None] * position_block[1][None, :]
    phase = phase + numbers[2][:, None] * position_block[2][None, :]
    phase = TWO_PI * phase
    return (jnp.cos(phase).astype(jnp.bfloat16), jnp.sin(phase).astype(jnp.bfloat16))


def contract(left, right):
    return lax.dot_general(
        left, right, (((1,), (1,)), ((), ())), preferred_element_type=jnp.float32
    )


def amplitude_term(moment_block, position_block, weight_block):
    cosine, sine = tables(moment_block, position_block)
    return jnp.concatenate([contract(weight_block, cosine), contract(weight_block, sine)], 0)


def gradient_term(adjoint_block, moment_block, position_block):
    cosine, sine = tables(moment_block, position_block)
    bin_count = adjoint_block.shape[0] // 2
    return jnp.dot(adjoint_block[:bin_count], cosine, preferred_element_type=jnp.float32) + jnp.dot(
        adjoint_block[bin_count:], sine, preferred_element_type=jnp.float32
    )


def couple(cotangent, real_one, imag_one, real_two, imag_two):
    real_part = cotangent * (real_one * real_two - imag_one * imag_two)
    imag_part = -cotangent * (imag_one * real_two + real_one * imag_two)
    return jnp.concatenate([real_part, imag_part], 0)


def triplet_terms(amplitude, triplets, cotangent, bin_count):
    real_rows = amplitude[:bin_count]
    imag_rows = amplitude[bin_count:]
    real_a = real_rows[:, triplets[0]]
    real_b = real_rows[:, triplets[1]]
    real_c = real_rows[:, triplets[2]]
    imag_a = imag_rows[:, triplets[0]]
    imag_b = imag_rows[:, triplets[1]]
    imag_c = imag_rows[:, triplets[2]]
    correlation = (
        real_a * real_b * real_c
        - real_a * imag_b * imag_c
        - imag_a * real_b * imag_c
        - imag_a * imag_b * real_c
    )
    adjoint = jnp.zeros(amplitude.shape, jnp.float32)
    adjoint = adjoint.at[:, triplets[0]].add(couple(cotangent, real_b, imag_b, real_c, imag_c))
    adjoint = adjoint.at[:, triplets[1]].add(couple(cotangent, real_a, imag_a, real_c, imag_c))
    adjoint = adjoint.at[:, triplets[2]].add(couple(cotangent, real_a, imag_a, real_b, imag_b))
    return (correlation, adjoint)


def spread(owned_part):
    return lax.all_gather(owned_part, "cell", axis=1, tiled=True)


def on_device(momenta, positions, weights, triplets, cotangent):
    devices = lax.axis_size("cell")
    bin_count = weights.shape[0]
    moment_count = momenta.shape[1]
    local_cells = positions.shape[1]
    all_cells = local_cells * devices
    norm_factor = 1.0 / math.sqrt(all_cells)
    moment_step = min(moment_count, 4096)
    moment_blocks = moment_count // moment_step
    full_amp = None

    def forward_cells(index, buffer):
        start = index * moment_step
        moment_block = lax.dynamic_slice_in_dim(momenta, start, moment_step, 1)
        term = amplitude_term(moment_block, positions, weights)
        return lax.dynamic_update_slice_in_dim(buffer, term, start, 1)

    partial_sums = lax.fori_loop(
        0, moment_blocks, forward_cells, jnp.zeros((2 * bin_count, moment_count), jnp.float32)
    )
    owned_amp = (
        lax.psum_scatter(partial_sums, "cell", scatter_dimension=1, tiled=True) * norm_factor
    )
    amplitude = spread(owned_amp)
    correlation, adjoint = triplet_terms(amplitude, triplets, cotangent, bin_count)
    owned_sum = lax.psum_scatter(adjoint, "cell", scatter_dimension=1, tiled=True)
    owned_adjoint = (owned_sum * norm_factor).astype(jnp.bfloat16)
    full_adjoint = lax.all_gather(owned_adjoint, "cell", axis=1, tiled=True)

    def backward_cells(index, summed):
        start = index * moment_step
        moment_block = lax.dynamic_slice_in_dim(momenta, start, moment_step, 1)
        adjoint_block = lax.dynamic_slice_in_dim(full_adjoint, start, moment_step, 1)
        return summed + gradient_term(adjoint_block, moment_block, positions)

    weight_grad = lax.fori_loop(
        0, moment_blocks, backward_cells, jnp.zeros((bin_count, local_cells), jnp.float32)
    )
    return (correlation, weight_grad)


def solution(mesh):
    placed = (
        P(),
        P(None, ("grp", "cell")),
        P(None, ("grp", "cell")),
        P(None, ("grp", "cell")),
        P(None, ("grp", "cell")),
    )
    return jax.shard_map(
        on_device,
        mesh=mesh,
        in_specs=placed,
        out_specs=(P(None, ("grp", "cell")), P(None, ("grp", "cell"))),
        check_vma=False,
    )
```

profile of v0, /device:TPU:0, one launch (start us, length us, event | category | flops | bytes accessed | tf_op | source)
XLA Modules:
  0.0 1721.1 jit_solution(12182722601391225925)
XLA Ops:
  9.6 271.4 %while.27 = (s32[]{:T(128)}, f32[16,65536]{1,0:T(8,128)}, s32[3,65536]{1,0:T(4,128)}, f32[3,128]{1,0:T(4,128)S(1)}, bf16[8,128]{1,0:T(8,128)(2,1)S(1)}, /*index=5*/s32[]{:T(128)}, s32[]{:T(128)}, s32[]{:T(128)}, s32[]{:T(128)}) while((s32[]{:T(128)}, f32[16,65536]{1,0:T(8,128)}, s32[3,65536]{1,0:T(4,128)}, f32[3,128]{1,0:T(4,128)S(1)}, ...), condition=%wide.region_1.0_spmd, body=%wide.region_0.0_spmd.sunk | while | flops 24195076 | bytes 1091739 | solution.py:87
  10.5 7.7 convolution_bitcast_fusion.4
  27.4 7.7 convolution_bitcast_fusion.4
  44.4 7.7 convolution_bitcast_fusion.4
  61.4 7.7 convolution_bitcast_fusion.4
  78.3 7.7 convolution_bitcast_fusion.4
  95.3 7.7 convolution_bitcast_fusion.4
  112.3 7.7 convolution_bitcast_fusion.4
  129.2 7.7 convolution_bitcast_fusion.4
  146.1 7.7 convolution_bitcast_fusion.4
  163.1 7.7 convolution_bitcast_fusion.4
  180.0 7.7 convolution_bitcast_fusion.4
  197.0 7.7 convolution_bitcast_fusion.4
  214.0 7.7 convolution_bitcast_fusion.4
  264.8 7.7 convolution_bitcast_fusion.4
  281.0 16.9 copy.53
  298.0 333.3 %reduce-scatter.3.cloned.1.call-done = f32[16,4096]{0,1:T(8,128)} async-done(((f32[16,65536]{0,1:T(8,128)}), f32[16,4096]{0,1:T(8,128)}) %reduce-scatter.3.cloned.1.call-update) | async-done | bytes 262160 | tf_op jit(solution)/shard_map/reduce_scatter | solution.py:91
  635.2 166.6 %all-gather.3.cloned.1.call-done = f32[16,65536]{0,1:T(8,128)} async-done(((f32[16,4096]{0,1:T(8,128)}), f32[16,65536]{0,1:T(8,128)}) %all-gather.3.cloned.1.call-update) | async-done | bytes 4194320 | tf_op jit(solution)/shard_map/all_gather | solution.py:67
  801.8 44.5 %fusion.44 = (f32[8,65536]{0,1:T(8,128)}, f32[8,65536]{0,1:T(8,128)}) fusion(f32[16,65536]{0,1:T(8,128)} %all-gather.3.cloned.1.call-done), kind=kLoop, calls=%fused_computation.100 | loop fusion | bytes 8388608 | tf_op jit(solution)/shard_map/slice | solution.py:45
  846.3 11.6 gather_fusion.1
  857.9 11.6 gather_fusion
  869.5 11.6 gather_fusion.3
  881.0 11.6 gather_fusion.5
  892.6 11.6 gather_fusion.4
  904.2 11.6 gather_fusion.2
  917.2 15.4 scatter_custom_fusion
  932.9 24.6 %scatter_fusion = f32[16,65536]{0,1:T(8,128)} fusion(f32[16,65536]{0,1:T(8,128)} %scatter_custom_fusion, s32[512]{0:T(512)S(1)} %bitcast.180, f32[512,16]{1,0:T(8,128)S(1)} %copy.61), kind=kCustom, calls=%fused_computation.7 | custom fusion | flops 8192 | bytes 100352 | tf_op jit(solution)/shard_map/scatter-add | solution.py:61
  957.5 24.6 %scatter_fusion.1 = f32[16,65536]{0,1:T(8,128)} fusion(f32[16,65536]{0,1:T(8,128)} %scatter_fusion, s32[512]{0:T(512)S(1)} %bitcast.178, f32[512,16]{1,0:T(8,128)S(1)} %copy.62), kind=kCustom, calls=%fused_computation.8 | custom fusion | flops 8192 | bytes 100352 | tf_op jit(solution)/shard_map/scatter-add | solution.py:62
  982.1 330.6 %reduce-scatter.5.cloned.1.call-done = f32[16,4096]{0,1:T(8,128)} async-done(((f32[16,65536]{0,1:T(8,128)}), f32[16,4096]{0,1:T(8,128)}) %reduce-scatter.5.cloned.1.call-update) | async-done | bytes 262160 | tf_op jit(solution)/shard_map/reduce_scatter | solution.py:95
  1315.5 125.7 %all-gather.5.cloned.1.call-done = bf16[16,65536]{0,1:T(8,128)(2,1)} async-done(((bf16[16,4096]{0,1:T(8,128)(2,1)}), bf16[16,65536]{0,1:T(8,128)(2,1)}) %all-gather.5.cloned.1.call-update) | async-done | bytes 2097168 | tf_op jit(solution)/shard_map/all_gather | solution.py:97
  1441.2 12.8 copy.63
  1454.0 259.5 %while.28 = (s32[]{:T(128)}, f32[8,128]{1,0:T(8,128)S(1)}, bf16[16,65536]{1,0:T(8,128)(2,1)S(1)}, s32[3,65536]{1,0:T(4,128)}, f32[3,128]{1,0:T(4,128)S(1)}, /*in...) while((s32[]{:T(128)}, f32[8,128]{1,0:T(8,128)S(1)}, bf16[16,65536]{1,0:T(8,128)(2,1)S(1)}, ...), condition=%wide.region_8.0_spmd.clone, body=%wide.region_7.0_spmd.clone.sunk | while | flops 24132616 | bytes 448705 | solution.py:105
  (200 shorter events, 433.9 us)
Async XLA Ops:
  7.2 624.1 %reduce-scatter.3.cloned.1.call-start = ((), (), s32[]{:S(2)}) async-start(), calls=%async_computation.2 | async-start | bytes 35651584 | tf_op jit(solution)/shard_map/reduce_scatter | solution.py:91
  7.2 2.4 copy-start
  7.2 2.4 copy-start.3
  297.9 503.9 %all-gather.3.cloned.1.call-start = ((), (), s32[]{:S(2)}) async-start(), calls=%async_computation.3 | async-start | bytes 35651584 | tf_op jit(solution)/shard_map/all_gather | solution.py:67
  634.5 0.7 copy-start.2
  634.5 678.3 %reduce-scatter.5.cloned.1.call-start = ((), (), s32[]{:S(2)}) async-start(), calls=%async_computation.4 | async-start | bytes 35651584 | tf_op jit(solution)/shard_map/reduce_scatter | solution.py:95
  846.3 70.1 %copy-start.1 = (f32[8,512]{1,0:T(8,128)S(1)}, f32[8,512]{1,0:T(8,128)}, u32[]{:S(2)}) copy-start(f32[8,512]{1,0:T(8,128)} %param.13) | copy-start | bytes 49156
  982.1 459.1 %all-gather.5.cloned.1.call-start = ((), (), s32[]{:S(2)}) async-start(), calls=%async_computation.5 | async-start | bytes 17825792 | tf_op jit(solution)/shard_map/all_gather | solution.py:97
  1713.6 0.6 copy-start.4
Sparse Core Ops, SparseCore 0:
  298.0 333.2 reduce-scatter.2
  634.6 167.1 all-gather.2
  982.2 330.5 reduce-scatter.4
  1315.7 125.5 all-gather.4
where the time goes:
time: 1730 us; the launch traced here: 1720 us
  waiting for transfers between devices  956 us (55%)
  matrix products  490 us (28%)
  local copies, waits for them, and re-layouts  149 us (9%)
  other arithmetic  110 us (6%)
    reduce_scatter x1, waiting for transfers between devices, on_device(): lax.psum_scatter(partial_sums, 'cell', scatter_dimension=1, tiled=True)  333 us
    reduce_scatter x1, waiting for transfers between devices, on_device(): lax.psum_scatter(adjoint, 'cell', scatter_dimension=1, tiled=True)  331 us
    dot_general x32, matrix products, contract(): lax.dot_general(left, right, (((1,), (1,)), ((), ())), preferred_element_...  245 us
    all_gather x1, waiting for transfers between devices, spread(): return lax.all_gather(owned_part, 'cell', axis=1, tiled=True)  167 us
    all_gather x1, waiting for transfers between devices, on_device(): full_adjoint = lax.all_gather(owned_adjoint, 'cell', axis=1, tiled=True)  126 us
    dot_general x16, matrix products, gradient_term(): jnp.dot(adjoint_block[bin_count:], sine, preferred_element_type=jnp.float32)  123 us
    dot_general x16, matrix products, gradient_term(): jnp.dot(adjoint_block[:bin_count], cosine, preferred_element_type=jnp.flo...  122 us
    slice x1, local copies, waits for them, and re-layouts, triplet_terms(): real_rows = amplitude[:bin_count]  44.5 us
  transfers between devices with their start and end apart: 4, of which 4 were waited for; matrix products, arithmetic and copies ran while one was open for 0% of the time, Pallas kernels for 0%

commit v1 on v0

--- a/solution.py
+++ b/solution.py
@@ -5,6 +5,18 @@
 from jax.sharding import PartitionSpec as P
 
 TWO_PI = 2.0 * math.pi
+
+
+def collect(shard, axis, dim):
+    ways, here = (lax.axis_size(axis), lax.axis_index(axis))
+    grown, reach = (shard, 1)
+    while reach < ways:
+        theirs = lax.ppermute(grown, axis, [(d, d ^ reach) for d in range(ways)])
+        mine_first = jnp.concatenate([grown, theirs], axis=dim)
+        theirs_first = jnp.concatenate([theirs, grown], axis=dim)
+        grown = jnp.where(here & reach == 0, mine_first, theirs_first)
+        reach = 2 * reach
+    return grown
 
 
 def tables(moment_block, position_block):
@@ -94,7 +106,7 @@
     correlation, adjoint = triplet_terms(amplitude, triplets, cotangent, bin_count)
     owned_sum = lax.psum_scatter(adjoint, "cell", scatter_dimension=1, tiled=True)
     owned_adjoint = (owned_sum * norm_factor).astype(jnp.bfloat16)
-    full_adjoint = lax.all_gather(owned_adjoint, "cell", axis=1, tiled=True)
+    full_adjoint = collect(owned_adjoint, "cell", 1)
 
     def backward_cells(index, summed):
         start = index * moment_step

time: 1730 us -> 1030 us (0.60)
  waiting for transfers between devices: 956 us -> 264 us
  local copies, waits for them, and re-layouts: 149 us -> 130 us
    reduce_scatter x1, waiting for transfers between devices: 331 us -> 71.4 us  [on_device(): lax.psum_scatter(adjoint, 'cell', scatter_dimension=1, tiled=True)]
    reduce_scatter x1, waiting for transfers between devices: 333 us -> 75.6 us  [on_device(): lax.psum_scatter(partial_sums, 'cell', scatter_dimension=1, tiled=True)]
    all_gather x1 -> x0, waiting for transfers between devices: 126 us -> none  [on_device(): full_adjoint = lax.all_gather(owned_adjoint, 'cell', axis=1, tiled=True)]
    all_gather x1, waiting for transfers between devices: 167 us -> 49.8 us  [spread(): return lax.all_gather(owned_part, 'cell', axis=1, tiled=True)]
    ppermute x0 -> x4, waiting for transfers between devices: none -> 67.2 us  [collect(): theirs = lax.ppermute(grown, axis, [(d, d ^ reach) for d in range(ways)])]
    slice x1 -> x2, local copies, waits for them, and re-layouts: 44.5 us -> 20.1 us  [triplet_terms(): real_rows = amplitude[:bin_count]]
    scatter-add x0 -> x1, local copies, waits for them, and re-layouts: none -> 19.1 us  [triplet_terms(): adjoint.at[:, triplets[2]]]
  transfers between devices with their start and end apart: 4 -> 7, of which waited for: 4 -> 7; matrix products, arithmetic and copies ran while one was open for 0% -> 0% of each run, Pallas kernels for 0% -> 0%
where the time goes in v1:
time: 1030 us; the launch traced here: 1010 us
  matrix products  490 us (48%)
  waiting for transfers between devices  264 us (26%)
  local copies, waits for them, and re-layouts  130 us (13%)
  other arithmetic  109 us (11%)
  between operations  14.3 us (1%)
    dot_general x32, matrix products, contract(): lax.dot_general(left, right, (((1,), (1,)), ((), ())), preferred_element_...  245 us
    dot_general x16, matrix products, gradient_term(): jnp.dot(adjoint_block[bin_count:], sine, preferred_element_type=jnp.float32)  123 us
    dot_general x16, matrix products, gradient_term(): jnp.dot(adjoint_block[:bin_count], cosine, preferred_element_type=jnp.flo...  122 us
    reduce_scatter x1, waiting for transfers between devices, on_device(): lax.psum_scatter(partial_sums, 'cell', scatter_dimension=1, tiled=True)  75.6 us
    reduce_scatter x1, waiting for transfers between devices, on_device(): lax.psum_scatter(adjoint, 'cell', scatter_dimension=1, tiled=True)  71.4 us
    ppermute x4, waiting for transfers between devices, collect(): theirs = lax.ppermute(grown, axis, [(d, d ^ reach) for d in range(ways)])  67.2 us
    all_gather x1, waiting for transfers between devices, spread(): return lax.all_gather(owned_part, 'cell', axis=1, tiled=True)  49.8 us
    convert_element_type x32, other arithmetic, tables(): numbers = moment_block.astype(jnp.float32)  27.3 us
  transfers between devices with their start and end apart: 7, of which 7 were waited for; matrix products, arithmetic and copies ran while one was open for 0% of the time, Pallas kernels for 0%

profile of v1, /device:TPU:0, one launch (start us, length us, event | category | flops | bytes accessed | tf_op | source)
XLA Modules:
  0.0 1011.6 jit_solution(5152646143350467079)
XLA Ops:
  9.5 271.3 %while.27 = (s32[]{:T(128)}, f32[16,65536]{1,0:T(8,128)}, s32[3,65536]{1,0:T(4,128)}, f32[3,128]{1,0:T(4,128)S(1)}, bf16[8,128]{1,0:T(8,128)(2,1)S(1)}, /*index=5*/s32[]{:T(128)}, s32[]{:T(128)}, s32[]{:T(128)}, s32[]{:T(128)}) while((s32[]{:T(128)}, f32[16,65536]{1,0:T(8,128)}, s32[3,65536]{1,0:T(4,128)}, f32[3,128]{1,0:T(4,128)S(1)}, ...), condition=%wide.region_1.0_spmd, body=%wide.region_0.0_spmd.sunk | while | flops 24195076 | bytes 1091731 | solution.py:99
  18.0 7.7 convolution_bitcast_fusion.4
  34.9 7.7 convolution_bitcast_fusion.4
  51.9 7.7 convolution_bitcast_fusion.4
  85.8 7.7 convolution_bitcast_fusion.4
  102.7 7.7 convolution_bitcast_fusion.4
  119.6 7.7 convolution_bitcast_fusion.4
  136.6 7.7 convolution_bitcast_fusion.4
  170.5 7.7 convolution_bitcast_fusion.4
  204.4 7.7 convolution_bitcast_fusion.4
  221.3 7.7 convolution_bitcast_fusion.4
  238.3 7.7 convolution_bitcast_fusion.4
  255.3 7.7 convolution_bitcast_fusion.4
  280.9 75.6 %reduce-scatter.3.cloned.1.call-done = f32[16,4096]{1,0:T(8,128)} async-done(((f32[16,65536]{1,0:T(8,128)}), f32[16,4096]{1,0:T(8,128)}) %reduce-scatter.3.cloned.1.call-update) | async-done | bytes 262160 | tf_op jit(solution)/shard_map/reduce_scatter | solution.py:103
  358.3 49.8 %all-gather.2.cloned.1.call-done = f32[16,65536]{1,0:T(8,128)} async-done(((f32[16,4096]{1,0:T(8,128)}), f32[16,65536]{1,0:T(8,128)}) %all-gather.2.cloned.1.call-update) | async-done | bytes 4194320 | tf_op jit(solution)/shard_map/all_gather | solution.py:79
  411.9 16.3 %copy.55 = f32[8,65536]{0,1:T(8,128)} copy(f32[8,65536]{1,0:T(8,128)} %get-tuple-element.278) | data formatting | bytes 4194304 | tf_op jit(solution)/shard_map/slice | solution.py:57
  428.2 11.6 %gather_fusion.1 = f32[512,8]{1,0:T(8,128)S(1)} fusion(f32[8,65536]{0,1:T(8,128)} %copy.55, s32[1024]{0:T(1024)S(1)} %pad_clamp_fusion.1), kind=kCustom, calls=%fused_computation.1 | custom fusion | bytes 34816 | tf_op jit(solution)/shard_map/gather | solution.py:60
  439.8 11.6 %gather_fusion.2 = f32[512,8]{1,0:T(8,128)S(1)} fusion(f32[8,65536]{0,1:T(8,128)} %copy.55, s32[1024]{0:T(1024)S(1)} %pad_clamp_fusion), kind=kCustom, calls=%fused_computation.2 | custom fusion | bytes 34816 | tf_op jit(solution)/shard_map/gather | solution.py:61
  451.4 16.5 %copy.61 = f32[8,65536]{0,1:T(8,128)} copy(f32[8,65536]{1,0:T(8,128)S(1)} %get-tuple-element.279) | data formatting | bytes 4194304 | tf_op jit(solution)/shard_map/slice | solution.py:58
  467.9 11.6 %gather_fusion.3 = f32[512,8]{1,0:T(8,128)S(1)} fusion(f32[8,65536]{0,1:T(8,128)} %copy.61, s32[1024]{0:T(1024)S(1)} %pad_clamp_fusion.1), kind=kCustom, calls=%fused_computation.3 | custom fusion | bytes 34816 | tf_op jit(solution)/shard_map/gather | solution.py:63
  479.5 11.6 %gather_fusion.4 = f32[512,8]{1,0:T(8,128)S(1)} fusion(f32[8,65536]{0,1:T(8,128)} %copy.61, s32[1024]{0:T(1024)S(1)} %pad_clamp_fusion), kind=kCustom, calls=%fused_computation.4 | custom fusion | bytes 34816 | tf_op jit(solution)/shard_map/gather | solution.py:64
  491.1 11.6 %gather_fusion = f32[512,8]{1,0:T(8,128)S(1)} fusion(f32[8,65536]{0,1:T(8,128)} %copy.55, s32[1024]{0:T(1024)S(1)} %pad_clamp_fusion.2), kind=kCustom, calls=%fused_computation | custom fusion | bytes 34816 | tf_op jit(solution)/shard_map/gather | solution.py:59
  502.7 11.6 %gather_fusion.5 = f32[512,8]{1,0:T(8,128)S(1)} fusion(f32[8,65536]{0,1:T(8,128)} %copy.61, s32[1024]{0:T(1024)S(1)} %pad_clamp_fusion.2), kind=kCustom, calls=%fused_computation.5 | custom fusion | bytes 34816 | tf_op jit(solution)/shard_map/gather | solution.py:62
  515.6 15.4 %scatter_custom_fusion = f32[16,65536]{0,1:T(8,128)} fusion(s32[512]{0:T(512)S(1)} %bitcast.182, f32[512,16]{1,0:T(8,128)S(1)} %copy.67, f32[]{:T(128)} %constant.82.clone.1), kind=kCustom, calls=%fused_computation.56 | custom fusion | flops 8192 | bytes 4194308 | tf_op jit(solution)/shard_map/scatter-add | solution.py:72
  531.3 24.6 %scatter_fusion = f32[16,65536]{0,1:T(8,128)} fusion(f32[16,65536]{0,1:T(8,128)} %scatter_custom_fusion, s32[512]{0:T(512)S(1)} %bitcast.180, f32[512,16]{1,0:T(8,128)S(1)} %copy.68), kind=kCustom, calls=%fused_computation.7 | custom fusion | flops 8192 | bytes 100352 | tf_op jit(solution)/shard_map/scatter-add | solution.py:73
  555.9 24.6 %scatter_fusion.1 = f32[16,65536]{0,1:T(8,128)} fusion(f32[16,65536]{0,1:T(8,128)} %scatter_fusion, s32[512]{0:T(512)S(1)} %bitcast.178, f32[512,16]{1,0:T(8,128)S(1)} %copy.69), kind=kCustom, calls=%fused_computation.8 | custom fusion | flops 8192 | bytes 100352 | tf_op jit(solution)/shard_map/scatter-add | solution.py:74
  580.5 19.1 %copy.70 = f32[16,65536]{1,0:T(8,128)} copy(f32[16,65536]{0,1:T(8,128)} %scatter_fusion.1) | data formatting | bytes 8388608 | tf_op jit(solution)/shard_map/scatter-add | solution.py:74
  599.6 71.4 %reduce-scatter.5.cloned.1.call-done = f32[16,4096]{1,0:T(8,128)} async-done(((f32[16,65536]{1,0:T(8,128)}), f32[16,4096]{1,0:T(8,128)}) %reduce-scatter.5.cloned.1.call-update) | async-done | bytes 262160 | tf_op jit(solution)/shard_map/reduce_scatter | solution.py:107
  674.1 7.9 collective-permute-done.1
  683.0 12.3 %collective-permute-done.2 = bf16[16,16384]{1,0:T(8,128)(2,1)S(1)} collective-permute-done((bf16[16,16384]{1,0:T(8,128)(2,1)S(1)}, bf16[16,16384]{1,0:T(8,128)(2,1)S(1)}, u32[]{:S(2)}, u32[]{:S(2)}) %collective-permute-start.2) | collective-permute-done | bytes 524320 | tf_op jit(solution)/shard_map/ppermute | solution.py:14
  696.9 45.7 %collective-permute-done.3 = bf16[16,32768]{1,0:T(8,128)(2,1)} collective-permute-done((bf16[16,32768]{1,0:T(8,128)(2,1)S(1)}, bf16[16,32768]{1,0:T(8,128)(2,1)}, u32[]{:S(2)}, u32[]{:S(2)}) %collective-permute-start.3) | collective-permute-done | bytes 1048608 | tf_op jit(solution)/shard_map/ppermute | solution.py:14
  744.6 259.6 %while.28 = (s32[]{:T(128)}, f32[8,128]{1,0:T(8,128)S(1)}, bf16[16,65536]{1,0:T(8,128)(2,1)S(1)}, s32[3,65536]{1,0:T(4,128)}, f32[3,128]{1,0:T(4,128)S(1)}, /*in...) while((s32[]{:T(128)}, f32[8,128]{1,0:T(8,128)S(1)}, bf16[16,65536]{1,0:T(8,128)(2,1)S(1)}, ...), condition=%wide.region_8.9_spmd.clone, body=%wide.region_7.8_spmd.clone.sunk | while | flops 24132616 | bytes 448697 | solution.py:117
  (210 shorter events, 455.3 us)
Async XLA Ops:
  7.2 349.3 %reduce-scatter.3.cloned.1.call-start = ((), (), s32[]{:S(2)}) async-start(), calls=%async_computation.2 | async-start | bytes 4456448 | tf_op jit(solution)/shard_map/reduce_scatter | solution.py:103
  7.2 2.2 copy-start
  7.2 2.2 copy-start.3
  280.8 77.4 %copy-start.2 = (s32[3,512]{1,0:T(4,128)S(1)}, s32[3,512]{1,0:T(4,128)}, u32[]{:S(2)}) copy-start(s32[3,512]{1,0:T(4,128)} %param.12) | copy-start | bytes 18436
  280.8 127.3 %all-gather.2.cloned.1.call-start = ((), (), s32[]{:S(2)}) async-start(), calls=%async_computation.3 | async-start | bytes 4456448 | tf_op jit(solution)/shard_map/all_gather | solution.py:79
  358.2 312.9 %reduce-scatter.5.cloned.1.call-start = ((), (), s32[]{:S(2)}) async-start(), calls=%async_computation.4 | async-start | bytes 4456448 | tf_op jit(solution)/shard_map/reduce_scatter | solution.py:107
  467.9 47.0 %copy-start.1 = (f32[8,512]{1,0:T(8,128)S(1)}, f32[8,512]{1,0:T(8,128)}, u32[]{:S(2)}) copy-start(f32[8,512]{1,0:T(8,128)} %param.13) | copy-start | bytes 49156
  672.0 1.4 collective-permute-start
  673.5 8.4 collective-permute-start.1
  682.1 13.2 %collective-permute-start.2 = (bf16[16,16384]{1,0:T(8,128)(2,1)S(1)}, bf16[16,16384]{1,0:T(8,128)(2,1)S(1)}, u32[]{:S(2)}, u32[]{:S(2)}) collective-permute-start(bf16[16,16384]{1,0:T(8,128)(2,1)S(1)} %maximum_select_fusion.2), channel_id=1, source_target_pairs={{0,4},{1,5},{2,6},{3,7},{4,0},{5,1},{6,2},{7,3},{8,12},{9,13},{10,... | collective-permute-start | bytes 1572872 | tf_op jit(solution)/shard_map/ppermute | solution.py:14
  695.5 47.0 %collective-permute-start.3 = (bf16[16,32768]{1,0:T(8,128)(2,1)S(1)}, bf16[16,32768]{1,0:T(8,128)(2,1)}, u32[]{:S(2)}, u32[]{:S(2)}) collective-permute-start(bf16[16,32768]{1,0:T(8,128)(2,1)S(1)} %maximum_select_fusion.1), channel_id=1, source_target_pairs={{0,8},{1,9},{2,10},{3,11},{4,12},{5,13},{6,14},{7,15},{8,0},{9,1},... | collective-permute-start | bytes 3145736 | tf_op jit(solution)/shard_map/ppermute | solution.py:14
  1004.1 0.6 copy-start.4
Sparse Core Ops, SparseCore 0:
  280.9 75.4 reduce-scatter.2
  358.6 49.4 all-gather.1
  599.7 71.2 reduce-scatter.4
